TPU v7x, 32 devices: a whole 2x2x4 slice. The times are simulated.
32 devices in a mesh: gx: 4 (over z), gy: 4 (over y, x), gz: 2 (over core).
Axes of the slice: x: 2, y: 2, z: 4, core: 2. Of those that a mesh axis runs over, the one named last changes fastest.
Arguments:
- species_field: float32 [8, 384, 6144], P('gz', 'gx', 'gy'), may hold values from -24 to 24
- start_first: float32 [384, 96], replicated, may hold values from -0.3125 to 0.3125
- start_second: float32 [384, 96], replicated, may hold values from -0.3125 to 0.3125
Outputs:
- factor_first: float32 [384, 96], replicated
- factor_second: float32 [384, 96], replicated
- core_tensor: float32 [16, 8, 96, 96], P('gx', 'gz', 'gy')
All inputs are finite; a program needn't handle non-finite values.
Results may differ from a plain program's by a relative error of at most 0.0003.
Values sent between devices are 32-bit elements; how exact they have to be, the bound alone decides.
A program may use at most 64 MiB of HBM per device.

v0:
```python
import jax
import jax.numpy as jnp
from jax import lax
from jax.sharding import PartitionSpec as P

S = 16
ITERS = 2
exact_precision = lax.Precision.HIGHEST


def leading(image_fn, start):
    current = start
    for turn in range(ITERS):
        images = image_fn(current)
        cross_gram = jnp.dot(images.T, images, precision=exact_precision)
        lower_factor = jnp.linalg.cholesky(cross_gram)
        current = lax.linalg.triangular_solve(
            lower_factor, images, left_side=False, lower=True, transpose_a=True
        )
    return current


def local(species_field, start_first, start_second):
    fibres = lax.all_to_all(species_field, "gx", split_axis=2, concat_axis=1, tiled=True)
    partial_gram = jnp.einsum("zic,zjc->ij", fibres, fibres, precision=exact_precision)
    gram_first = lax.psum(partial_gram, ("gx", "gy", "gz"))

    def image_first(current):
        return jnp.dot(gram_first, current, precision=exact_precision)

    factor_first = leading(image_first, start_first)
    cells = fibres.shape[2] // S
    blocks = fibres.reshape(fibres.shape[0], fibres.shape[1], cells, S)
    projected = jnp.einsum("ziks,ir->zrsk", blocks, factor_first, precision=exact_precision)
    rows_second = lax.all_to_all(
        lax.all_to_all(projected, "gx", split_axis=2, concat_axis=3, tiled=True),
        "gy",
        split_axis=1,
        concat_axis=3,
        tiled=True,
    )
    flat_rows = rows_second.reshape(-1, rows_second.shape[3])
    partial_second = jnp.dot(flat_rows.T, flat_rows, precision=exact_precision)
    gram_second = lax.psum(partial_second, ("gx", "gy", "gz"))

    def image_second(current):
        return jnp.dot(gram_second, current, precision=exact_precision)

    factor_second = leading(image_second, start_second)
    core_local = jnp.einsum("zrsj,jq->szrq", rows_second, factor_second, precision=exact_precision)
    return (factor_first, factor_second, core_local)


def solution(mesh):
    return jax.shard_map(
        local,
        mesh=mesh,
        in_specs=(P("gz", "gx", "gy"), P(), P()),
        out_specs=(P(), P(), P("gx", "gz", "gy", None)),
        check_vma=False,
    )
```

profile of v0, /device:TPU:0, one launch (start us, length us, event | category | flops | bytes accessed | tf_op | source)
XLA Modules:
  0.0 482.7 jit_solution(708190136586059608)
XLA Ops:
  7.2 0.0 copy-start
  7.2 0.0 all-reduce.3.cloned.1.call-start
  7.2 4.5 copy.38
  11.8 77.0 %all_to_all.54 = f32[4,96,1536]{1,0,2:T(4,128)S(1)} all-to-all(f32[4,96,1536]{1,0,2:T(4,128)} %copy.38), channel_id=1, replica_groups=mesh['gx'=4,'gy'=4,'gz'=2] {'gx'}, dimensions={2} | all-to-all | bytes 4718592 | tf_op jit(solution)/shard_map/all_to_all | solution.py:24
  88.8 2.8 copy.40
  91.5 7.1 %convolution_bitcast_fusion = f32[384,384]{1,0:T(8,128)} fusion(f32[4,384,384]{2,1,0:T(8,128)} %bitcast.105), kind=kOutput, calls=%fused_computation.4 | convolution fusion | flops 2717908992 | bytes 2949120 | tf_op jit(solution)/shard_map/zic,zjc->ij/dot_general | solution.py:25
  98.7 0.0 all-reduce.3.cloned.1.call-update
  98.7 0.0 all-reduce.5.cloned.1.call-start
  98.7 3.7 copy.63
  102.4 3.6 reshape.25
  106.0 120.4 %all-reduce.3.cloned.1.call-done = f32[384,384]{1,0:T(8,128)} async-done(((f32[384,384]{1,0:T(8,128)}), f32[384,384]{1,0:T(8,128)}) %all-reduce.3.cloned.1.call-update) | async-done | bytes 589840 | tf_op jit(solution)/shard_map/psum | solution.py:26
  226.4 0.0 copy-done
  226.4 1.9 fusion.23
  228.2 0.3 fusion.24
  228.6 0.1 copy.41
  228.7 8.8 %cholesky.74 = f32[96,96]{1,0:T(8,128)S(1)} custom-call(f32[96,96]{1,0:T(8,128)S(1)} %fusion.20), custom_call_target="Cholesky" | custom-call | tf_op jit(solution)/shard_map/jit(cholesky)/cholesky | solution.py:16
  237.5 0.6 compare_reduce_fusion.3
  238.1 0.7 fusion.7
  238.8 7.4 %custom-call.8 = f32[1,96,96]{1,2,0:T(8,128)S(1)} custom-call(f32[1,96,96]{2,1,0:T(8,128)S(1)} %fusion.7), custom_call_target="InvertDiagBlocksLowerTriangular" | custom-call | tf_op jit(solution)/shard_map/triangular_solve/custom-call.0 | solution.py:17
  246.2 0.3 convolution_bitcast_fusion.3
  246.5 0.7 fusion.25
  247.2 0.3 fusion.26
  247.6 0.1 copy.42
  247.7 8.8 %cholesky.85 = f32[96,96]{1,0:T(8,128)S(1)} custom-call(f32[96,96]{1,0:T(8,128)S(1)} %fusion.18), custom_call_target="Cholesky" | custom-call | tf_op jit(solution)/shard_map/jit(cholesky)/cholesky | solution.py:16
  256.5 0.6 compare_reduce_fusion.2
  257.2 0.7 fusion.8
  257.8 7.4 %custom-call.9 = f32[1,96,96]{1,2,0:T(8,128)S(1)} custom-call(f32[1,96,96]{2,1,0:T(8,128)S(1)} %fusion.8), custom_call_target="InvertDiagBlocksLowerTriangular" | custom-call | tf_op jit(solution)/shard_map/triangular_solve/custom-call.0 | solution.py:17
  265.2 0.3 fusion.16
  265.5 0.0 copy-start.3
  265.5 2.6 fusion.2
  268.2 0.1 copy.44
  268.3 23.2 %all_to_all.55 = f32[4,96,16,24]{1,3,0,2:T(8,128)S(1)} all-to-all(f32[4,96,16,24]{1,3,0,2:T(8,128)S(1)} %copy.44), channel_id=1, replica_groups=mesh['gx'=4,'gy'=4,'gz'=2] {'gx'}, dimensions={2} | all-to-all | bytes 1179648 | tf_op jit(solution)/shard_map/all_to_all | solution.py:36
  291.5 0.1 copy.46
  291.6 0.5 copy.47
  292.1 13.3 %all_to_all.56 = f32[4,96,4,96]{3,2,0,1:T(4,128)S(1)} all-to-all(f32[4,96,4,96]{3,2,0,1:T(4,128)S(1)} %copy.47), channel_id=1, replica_groups=mesh['gx'=4,'gy'=4,'gz'=2] {'gy'}, dimensions={1} | all-to-all | bytes 1179648 | tf_op jit(solution)/shard_map/all_to_all | solution.py:35
  305.4 0.3 copy.48
  305.6 0.2 copy.49
  305.8 0.4 reshape.26
  306.2 0.0 copy-start.5
  306.3 2.1 fusion.27
  308.4 0.0 all-reduce.5.cloned.1.call-update
  308.4 0.2 copy.52
  308.6 0.4 all_to_all.50
  309.0 126.3 %all-reduce.5.cloned.1.call-done = f32[384,384]{1,0:T(8,128)} async-done(((f32[384,384]{1,0:T(8,128)}), f32[384,384]{1,0:T(8,128)}) %all-reduce.5.cloned.1.call-update) | async-done | bytes 589840 | tf_op jit(solution)/shard_map/psum | solution.py:44
  435.3 1.9 fusion.28
  437.2 0.3 fusion.29
  437.5 0.1 copy.50
  437.6 8.8 %cholesky.96 = f32[96,96]{1,0:T(8,128)S(1)} custom-call(f32[96,96]{1,0:T(8,128)S(1)} %fusion.15), custom_call_target="Cholesky" | custom-call | tf_op jit(solution)/shard_map/jit(cholesky)/cholesky | solution.py:16
  446.4 0.6 compare_reduce_fusion.1
  447.1 0.7 fusion.9
  447.7 7.4 %custom-call.10 = f32[1,96,96]{1,2,0:T(8,128)S(1)} custom-call(f32[1,96,96]{2,1,0:T(8,128)S(1)} %fusion.9), custom_call_target="InvertDiagBlocksLowerTriangular" | custom-call | tf_op jit(solution)/shard_map/triangular_solve/custom-call.0 | solution.py:17
  455.1 0.3 convolution_bitcast_fusion.2
  455.5 0.7 fusion.30
  456.2 0.3 fusion.31
  456.5 0.1 copy.51
  456.6 8.8 %cholesky.107 = f32[96,96]{1,0:T(8,128)S(1)} custom-call(f32[96,96]{1,0:T(8,128)S(1)} %fusion.13), custom_call_target="Cholesky" | custom-call | tf_op jit(solution)/shard_map/jit(cholesky)/cholesky | solution.py:16
  465.5 0.6 compare_reduce_fusion
  466.1 0.7 fusion.10
  466.8 7.4 %custom-call.11 = f32[1,96,96]{1,2,0:T(8,128)S(1)} custom-call(f32[1,96,96]{2,1,0:T(8,128)S(1)} %fusion.10), custom_call_target="InvertDiagBlocksLowerTriangular" | custom-call | tf_op jit(solution)/shard_map/triangular_solve/custom-call.0 | solution.py:17
  474.1 0.3 fusion.11
  474.5 0.0 copy-start.4
  474.5 0.6 convolution_bitcast_fusion.1
  475.1 0.7 copy.53
  475.8 0.0 copy-done.4
  (14 shorter events, 0.2 us)
Async XLA Ops:
  7.2 219.2 %copy-start = (f32[384,96]{0,1:T(8,128)S(1)}, f32[384,96]{0,1:T(8,128)}, u32[]{:S(2)}) copy-start(f32[384,96]{0,1:T(8,128)} %param.7) | copy-start | bytes 442372
  7.2 219.2 %all-reduce.3.cloned.1.call-start = ((), (), s32[]{:S(2)}) async-start(), calls=%async_computation.3 | async-start | bytes 1179648 | tf_op jit(solution)/shard_map/psum | solution.py:26
  98.7 336.6 %all-reduce.5.cloned.1.call-start = ((), (), s32[]{:S(2)}) async-start(), calls=%async_computation.4 | async-start | bytes 1179648 | tf_op jit(solution)/shard_map/psum | solution.py:44
  226.4 20.1 %copy-start.1 = (f32[384,384]{1,0:T(8,128)S(1)}, f32[384,384]{1,0:T(8,128)}, u32[]{:S(2)}) copy-start(f32[384,384]{1,0:T(8,128)} %all-reduce.3.cloned.1.call-done) | copy-start | bytes 1769476
  265.5 2.8 copy-start.3
  306.2 129.1 %copy-start.5 = (f32[384,96]{0,1:T(8,128)S(1)}, f32[384,96]{0,1:T(8,128)}, u32[]{:S(2)}) copy-start(f32[384,96]{0,1:T(8,128)} %param.8) | copy-start | bytes 442372
  435.3 20.1 %copy-start.2 = (f32[384,384]{1,0:T(8,128)S(1)}, f32[384,384]{1,0:T(8,128)}, u32[]{:S(2)}) copy-start(f32[384,384]{1,0:T(8,128)} %all-reduce.5.cloned.1.call-done) | copy-start | bytes 1769476
  474.5 1.3 copy-start.4
Sparse Core Ops, SparseCore 0:
  98.8 127.5 all-reduce.2
  308.5 126.7 all-reduce.4
where the time goes:
time: 483 us
  waiting for transfers between devices  247 us (51%)
  blocking collectives  114 us (24%)
  other arithmetic  69.9 us (14%)
  matrix products  20.4 us (4%)
  local copies, waits for them, and re-layouts  17.7 us (4%)
  between operations  14.4 us (3%)
    psum x1, waiting for transfers between devices, local(): gram_second = lax.psum(partial_second, ('gx', 'gy', 'gz'))  126 us
    psum x1, waiting for transfers between devices, local(): gram_first = lax.psum(partial_gram, ('gx', 'gy', 'gz'))  120 us
    all_to_all x1, blocking collectives, local(): lax.all_to_all(species_field, 'gx', split_axis=2, concat_axis=1, tiled=True)  77 us
    another operation x12, other arithmetic, leading(): lower_factor = jnp.linalg.cholesky(cross_gram)  37.8 us
    another operation x8, other arithmetic, leading(): lax.linalg.triangular_solve(lower_factor, images, left_side=False, lower=...  32 us
    all_to_all x1, blocking collectives, local(): lax.all_to_all(projected, 'gx', split_axis=2, concat_axis=3, tiled=True)  23.2 us
    all_to_all x1, blocking collectives, local(): lax.all_to_all(lax.all_to_all(projected, 'gx', split_axis=2, concat_axis=...  13.3 us
  transfers between devices with their start and end apart: 2, of which 2 were waited for; matrix products, arithmetic and copies ran while one was open for 2% of the time, Pallas kernels for 0%

commit v1 on v0

--- a/solution.py
+++ b/solution.py
@@ -1,11 +1,24 @@
+import functools
 import jax
 import jax.numpy as jnp
 from jax import lax
 from jax.sharding import PartitionSpec as P
+from jax.lax import all_to_all, psum
 
 S = 16
 ITERS = 2
 exact_precision = lax.Precision.HIGHEST
+
+
+def save_clusters(frame, on_dim, dim_k):
+    found_now = psum(1, "gx")
+    all_values = jnp.split(frame, found_now, axis=on_dim)
+    current_value = jnp.stack(all_values, axis=0)
+    state_now = all_to_all(current_value, "gx", 0, 0)
+    return jnp.concatenate(state_now, axis=dim_k)
+
+
+keep_up_indices = functools.partial(save_clusters, on_dim=2, dim_k=1)
 
 
 def leading(image_fn, start):
@@ -21,7 +34,7 @@
 
 
 def local(species_field, start_first, start_second):
-    fibres = lax.all_to_all(species_field, "gx", split_axis=2, concat_axis=1, tiled=True)
+    fibres = keep_up_indices(species_field)
     partial_gram = jnp.einsum("zic,zjc->ij", fibres, fibres, precision=exact_precision)
     gram_first = lax.psum(partial_gram, ("gx", "gy", "gz"))
 

time: 483 us -> 458 us (0.948)
  blocking collectives: 114 us -> 96.5 us
  local copies, waits for them, and re-layouts: 17.7 us -> 11.4 us
    all_to_all x1, blocking collectives: 77 us -> 60 us  [save_clusters(): state_now = all_to_all(current_value, 'gx', 0, 0)]
    all_to_all x2 -> x0, local copies, waits for them, and re-layouts: 6.45 us -> none  [local(): lax.all_to_all(species_field, 'gx', split_axis=2, concat_axis=1, tiled=True)]
    another operation x0 -> x2, local copies, waits for them, and re-layouts: none -> 5.34 us  [the longest x1 3.54 us: local(): blocks = fibres.reshape(fibres.shape[0], fibres.shape[1], cells, S)]
  transfers between devices with their start and end apart: 2 -> 2, of which waited for: 2 -> 2; matrix products, arithmetic and copies ran while one was open for 2% -> 1% of each run, Pallas kernels for 0% -> 0%
where the time goes in v1:
time: 458 us
  waiting for transfers between devices  248 us (54%)
  blocking collectives  96.5 us (21%)
  other arithmetic  70.1 us (15%)
  matrix products  18.1 us (4%)
  between operations  14.4 us (3%)
  local copies, waits for them, and re-layouts  11.4 us (2%)
    psum x1, waiting for transfers between devices, local(): gram_second = lax.psum(partial_second, ('gx', 'gy', 'gz'))  126 us
    psum x1, waiting for transfers between devices, local(): gram_first = lax.psum(partial_gram, ('gx', 'gy', 'gz'))  121 us
    all_to_all x1, blocking collectives, save_clusters(): state_now = all_to_all(current_value, 'gx', 0, 0)  60 us
    another operation x12, other arithmetic, leading(): lower_factor = jnp.linalg.cholesky(cross_gram)  37.8 us
    another operation x8, other arithmetic, leading(): lax.linalg.triangular_solve(lower_factor, images, left_side=False, lower=...  32 us
    all_to_all x1, blocking collectives, local(): lax.all_to_all(projected, 'gx', split_axis=2, concat_axis=3, tiled=True)  23.2 us
    all_to_all x1, blocking collectives, local(): lax.all_to_all(lax.all_to_all(projected, 'gx', split_axis=2, concat_axis=...  13.3 us
  transfers between devices with their start and end apart: 2, of which 2 were waited for; matrix products, arithmetic and copies ran while one was open for 1% of the time, Pallas kernels for 0%

profile of v1, /device:TPU:0, one launch (start us, length us, event | category | flops | bytes accessed | tf_op | source)
XLA Modules:
  0.0 458.0 jit_solution(16885157511403022289)
XLA Ops:
  7.2 0.0 copy-start
  7.2 0.0 all-reduce.3.cloned.1.call-start
  7.2 1.8 slice_bitcast_fusion.3
  9.0 0.2 pad_maximum_fusion
  9.2 60.0 %all_to_all.41 = f32[4,4,96,384]{3,2,1,0:T(8,128)S(1)} all-to-all(f32[4,4,96,384]{3,2,1,0:T(8,128)S(1)} %pad_maximum_fusion), channel_id=1, replica_groups=mesh['gx'=4,'gy'=4,'gz'=2] {'gx'}, dimensions={0} | all-to-all | bytes 4718592 | tf_op jit(solution)/shard_map/all_to_all | solution.py:17
  69.2 0.2 copy.37
  69.3 4.8 %convolution_bitcast_fusion = f32[384,384]{1,0:T(8,128)} fusion(f32[4,384,384]{2,1,0:T(8,128)S(1)} %bitcast.108), kind=kOutput, calls=%fused_computation.4 | convolution fusion | flops 2717908992 | bytes 2949120 | tf_op jit(solution)/shard_map/zic,zjc->ij/dot_general | solution.py:38
  74.1 0.0 all-reduce.3.cloned.1.call-update
  74.1 0.0 all-reduce.5.cloned.1.call-start
  74.2 2.8 copy.40
  77.0 3.5 reshape_reshape.3
  80.5 121.2 %all-reduce.3.cloned.1.call-done = f32[384,384]{1,0:T(8,128)} async-done(((f32[384,384]{1,0:T(8,128)}), f32[384,384]{1,0:T(8,128)}) %all-reduce.3.cloned.1.call-update) | async-done | bytes 589840 | tf_op jit(solution)/shard_map/psum | solution.py:39
  201.7 1.9 fusion.23
  203.6 0.3 fusion.24
  203.9 0.1 copy.38
  204.1 8.8 %cholesky.74 = f32[96,96]{1,0:T(8,128)S(1)} custom-call(f32[96,96]{1,0:T(8,128)S(1)} %fusion.20), custom_call_target="Cholesky" | custom-call | tf_op jit(solution)/shard_map/jit(cholesky)/cholesky | solution.py:29
  212.9 0.6 compare_reduce_fusion.3
  213.5 0.7 fusion.7
  214.2 7.4 %custom-call.8 = f32[1,96,96]{1,2,0:T(8,128)S(1)} custom-call(f32[1,96,96]{2,1,0:T(8,128)S(1)} %fusion.7), custom_call_target="InvertDiagBlocksLowerTriangular" | custom-call | tf_op jit(solution)/shard_map/triangular_solve/custom-call.0 | solution.py:30
  221.5 0.3 convolution_bitcast_fusion.3
  221.9 0.0 copy-done.1
  221.9 0.7 fusion.25
  222.6 0.3 fusion.26
  223.0 0.1 copy.39
  223.1 8.8 %cholesky.85 = f32[96,96]{1,0:T(8,128)S(1)} custom-call(f32[96,96]{1,0:T(8,128)S(1)} %fusion.18), custom_call_target="Cholesky" | custom-call | tf_op jit(solution)/shard_map/jit(cholesky)/cholesky | solution.py:29
  231.9 0.6 compare_reduce_fusion.2
  232.5 0.7 fusion.8
  233.2 7.4 %custom-call.9 = f32[1,96,96]{1,2,0:T(8,128)S(1)} custom-call(f32[1,96,96]{2,1,0:T(8,128)S(1)} %fusion.8), custom_call_target="InvertDiagBlocksLowerTriangular" | custom-call | tf_op jit(solution)/shard_map/triangular_solve/custom-call.0 | solution.py:30
  240.5 0.3 fusion.16
  240.9 0.0 copy-start.3
  240.9 2.6 fusion.2
  243.6 0.1 copy.42
  243.7 23.2 %all_to_all.42 = f32[4,96,16,24]{1,3,0,2:T(8,128)S(1)} all-to-all(f32[4,96,16,24]{1,3,0,2:T(8,128)S(1)} %copy.42), channel_id=1, replica_groups=mesh['gx'=4,'gy'=4,'gz'=2] {'gx'}, dimensions={2} | all-to-all | bytes 1179648 | tf_op jit(solution)/shard_map/all_to_all | solution.py:49
  266.8 0.1 copy.44
  266.9 0.5 copy.45
  267.4 13.3 %all_to_all.43 = f32[4,96,4,96]{3,2,0,1:T(4,128)S(1)} all-to-all(f32[4,96,4,96]{3,2,0,1:T(4,128)S(1)} %copy.45), channel_id=1, replica_groups=mesh['gx'=4,'gy'=4,'gz'=2] {'gy'}, dimensions={1} | all-to-all | bytes 1179648 | tf_op jit(solution)/shard_map/all_to_all | solution.py:48
  280.8 0.3 copy.46
  281.0 0.2 copy.47
  281.2 0.4 reshape.29
  281.6 0.0 copy-start.5
  281.6 2.1 fusion.27
  283.8 0.0 all-reduce.5.cloned.1.call-update
  283.8 0.2 copy.50
  284.0 0.4 all_to_all.37
  284.4 126.3 %all-reduce.5.cloned.1.call-done = f32[384,384]{1,0:T(8,128)} async-done(((f32[384,384]{1,0:T(8,128)}), f32[384,384]{1,0:T(8,128)}) %all-reduce.5.cloned.1.call-update) | async-done | bytes 589840 | tf_op jit(solution)/shard_map/psum | solution.py:57
  410.7 1.9 fusion.28
  412.5 0.3 fusion.29
  412.9 0.1 copy.48
  413.0 8.8 %cholesky.96 = f32[96,96]{1,0:T(8,128)S(1)} custom-call(f32[96,96]{1,0:T(8,128)S(1)} %fusion.15), custom_call_target="Cholesky" | custom-call | tf_op jit(solution)/shard_map/jit(cholesky)/cholesky | solution.py:29
  421.8 0.6 compare_reduce_fusion.1
  422.4 0.7 fusion.9
  423.1 7.4 %custom-call.10 = f32[1,96,96]{1,2,0:T(8,128)S(1)} custom-call(f32[1,96,96]{2,1,0:T(8,128)S(1)} %fusion.9), custom_call_target="InvertDiagBlocksLowerTriangular" | custom-call | tf_op jit(solution)/shard_map/triangular_solve/custom-call.0 | solution.py:30
  430.5 0.3 convolution_bitcast_fusion.2
  430.8 0.7 fusion.30
  431.5 0.3 fusion.31
  431.9 0.1 copy.49
  432.0 8.8 %cholesky.107 = f32[96,96]{1,0:T(8,128)S(1)} custom-call(f32[96,96]{1,0:T(8,128)S(1)} %fusion.13), custom_call_target="Cholesky" | custom-call | tf_op jit(solution)/shard_map/jit(cholesky)/cholesky | solution.py:29
  440.8 0.6 compare_reduce_fusion
  441.4 0.7 fusion.10
  442.1 7.4 %custom-call.11 = f32[1,96,96]{1,2,0:T(8,128)S(1)} custom-call(f32[1,96,96]{2,1,0:T(8,128)S(1)} %fusion.10), custom_call_target="InvertDiagBlocksLowerTriangular" | custom-call | tf_op jit(solution)/shard_map/triangular_solve/custom-call.0 | solution.py:30
  449.5 0.3 fusion.11
  449.8 0.0 copy-start.4
  449.8 0.6 convolution_bitcast_fusion.1
  450.5 0.7 copy.51
  (15 shorter events, 0.2 us)
Async XLA Ops:
  7.2 194.6 %copy-start = (f32[384,96]{0,1:T(8,128)S(1)}, f32[384,96]{0,1:T(8,128)}, u32[]{:S(2)}) copy-start(f32[384,96]{0,1:T(8,128)} %param.7) | copy-start | bytes 442372
  7.2 194.6 %all-reduce.3.cloned.1.call-start = ((), (), s32[]{:S(2)}) async-start(), calls=%async_computation.3 | async-start | bytes 1179648 | tf_op jit(solution)/shard_map/psum | solution.py:39
  74.1 336.5 %all-reduce.5.cloned.1.call-start = ((), (), s32[]{:S(2)}) async-start(), calls=%async_computation.4 | async-start | bytes 1179648 | tf_op jit(solution)/shard_map/psum | solution.py:57
  201.7 20.1 %copy-start.1 = (f32[384,384]{1,0:T(8,128)S(1)}, f32[384,384]{1,0:T(8,128)}, u32[]{:S(2)}) copy-start(f32[384,384]{1,0:T(8,128)} %all-reduce.3.cloned.1.call-done) | copy-start | bytes 1769476
  240.9 2.8 copy-start.3
  281.6 129.0 %copy-start.5 = (f32[384,96]{0,1:T(8,128)S(1)}, f32[384,96]{0,1:T(8,128)}, u32[]{:S(2)}) copy-start(f32[384,96]{0,1:T(8,128)} %param.8) | copy-start | bytes 442372
  410.7 20.1 %copy-start.2 = (f32[384,384]{1,0:T(8,128)S(1)}, f32[384,384]{1,0:T(8,128)}, u32[]{:S(2)}) copy-start(f32[384,384]{1,0:T(8,128)} %all-reduce.5.cloned.1.call-done) | copy-start | bytes 1769476
  449.8 1.3 copy-start.4
Sparse Core Ops, SparseCore 0:
  74.3 127.4 all-reduce.2
  283.9 126.7 all-reduce.4
